TPU v7x, 32 devices: a whole 2x2x4 slice. The times are simulated.
32 devices in a mesh: grp: 4 (over y, x), dev: 8 (over z, core).
Axes of the slice: x: 2, y: 2, z: 4, core: 2. Of those that a mesh axis runs over, the one named last changes fastest.
Arguments:
- particles: float32 [128, 5, 128], P(('grp', 'dev')), as said below
- entropy: float32 [128, 128], P(('grp', 'dev')), may hold values from 0.5 to 2
- lists: int32 [128, 64], P(('grp', 'dev')), may hold values from 0 to 127, as said below
- counts: int32 [128], P(('grp', 'dev')), may hold values from 16 to 64, as said below
Outputs:
- density: float32 [128, 128], P(('grp', 'dev'))
- accel: float32 [128, 3, 128], P(('grp', 'dev'))
Inputs may be any that keep to these rules, and one draw needn't show every extreme that they name: lists[c, 0] = c; every id lies in the group of c or in one of the two groups next to it, counting groups of 32 cells around a loop. `counts`: each count is a multiple of 16. `particles`: coordinates in 0 to 1 within the group's slab, masses positive, smoothing lengths from 0.3 to 0.6.
All inputs are finite; a program needn't handle non-finite values.
Results may differ from a plain program's by a relative error of at most 0.0003.
Values sent between devices are 32-bit elements; how exact they have to be, the bound alone decides.
No kernel may reach another device: no remote copies, remote signals or barrier semaphores. Data moves between devices by JAX's collectives and lax.ppermute only.
A program may use at most 64 MiB of HBM per device.

v0:
```python
import functools
import math

import jax
import jax.numpy as jnp
from jax import lax
from jax.experimental import pallas as pl
from jax.experimental.pallas import tpu as pltpu
from jax.sharding import Mesh
from jax.sharding import PartitionSpec as P


NORM = 21.0 / (16.0 * math.pi)
TINY = 1e-30
ROWS = 8
BATCH = 16
CHUNK = 16
VMEM_LIMIT = 24 * 1024 * 1024


def split3(v):
    hi = v.astype(jnp.bfloat16).astype(jnp.float32)
    rest = v - hi
    mid = rest.astype(jnp.bfloat16).astype(jnp.float32)
    return hi, mid, rest - mid


def right_parts(v):
    hi, mid, low = split3(v)
    return jnp.concatenate([hi, mid, hi, low, hi, mid], axis=0)


def left_parts(v):
    hi, mid, low = split3(v)
    return jnp.concatenate([hi, hi, mid, hi, low, mid], axis=0)


def sum_parts(v):
    hi, mid, low = split3(v)
    return jnp.concatenate([hi, mid, low, jnp.zeros_like(low)], axis=0).astype(jnp.bfloat16)


def left_rows(v):
    row = lax.broadcasted_iota(jnp.int32, v.shape, 0)
    return jnp.where(row < 3, -2.0 * v, jnp.where(row == 3, v[4:5], jnp.where(row == 4, 1.0, 0.0)))


def right_rows(v, shift):
    row = lax.broadcasted_iota(jnp.int32, v.shape, 0)
    rows = jnp.where(row < 5, v, 0.0)
    if shift:
        rows = rows + jnp.where(
            row == 0, shift, jnp.where(row == 4, shift * (2.0 * v[0:1] + shift), 0.0)
        )
    return rows


def table_cells(refs, sizes, fn):
    _, depth, cores, own = sizes
    per_ref = depth * own
    for at, ref in enumerate(refs):
        shift = float(at // cores - 1)

        def step(i, carry, ref=ref, at=at, shift=shift):
            fn(at * per_ref + i, ref[i], shift)
            return carry

        lax.fori_loop(0, per_ref, step, 0, unroll=4)


def list_batches(own, counts, cell_of, slot_of):
    made = jnp.int32(0)
    for cell in range(own):

        def step(k, made, cell=cell):
            cell_of[made] = cell
            slot_of[made] = k * BATCH
            return made + 1

        made = lax.fori_loop(0, lax.div(counts[cell], BATCH), step, made)
    return made


def rows_kernel(particles, rows):
    x, y, z, mass, smooth = (particles[k] for k in range(5))
    x, y, z = x - 0.5, y - 0.5, z - 0.5
    made = (x, y, z, jnp.ones_like(x), x * x + y * y + z * z, mass, 1.0 / smooth, jnp.exp(jnp.log(mass) * 0.2))
    for cell in range(particles.shape[1]):
        rows[cell] = jnp.concatenate([m[cell : cell + 1] for m in made], axis=0)


def density_kernel(sizes, index, counts, own_ref, entropy, *rest):
    refs, (density, weight, table, nu_rows, left, total, ahead, cell_of, slot_of) = (
        rest[:-9],
        rest[-9:],
    )
    own = sizes[3]
    width = own_ref.shape[2]

    def fill(at, v, shift):
        nu = v[7:8]
        table[at] = right_parts((nu * nu) * right_rows(v, shift)).astype(jnp.bfloat16)
        nu_rows[at] = jnp.broadcast_to(nu, v.shape)

    table_cells(refs, sizes, fill)
    for cell in range(own):
        v = own_ref[cell]
        parts = left_parts((4.0 * (v[6:7] * v[6:7])) * left_rows(v))
        left[cell] = jnp.transpose(parts).astype(jnp.bfloat16)
    total[...] = jnp.zeros_like(total)
    batches = list_batches(own, counts, cell_of, slot_of)

    def slots(batch, pair):
        cell, slot = cell_of[batch], slot_of[batch] + 2 * pair
        return index[cell, slot], index[cell, slot + 1]

    def squares(batch, pair):
        first, second = slots(batch, pair)
        right = jnp.concatenate([table[first], table[second]], axis=1)
        return jnp.dot(left[cell_of[batch]], right, preferred_element_type=jnp.float32)

    for pair in range(BATCH // 2):
        ahead[pair] = squares(0, pair)

    def step(batch, carry):
        later = jnp.minimum(batch + 1, batches - 1)
        sums = [None] * (width // CHUNK)
        for pair in range(BATCH // 2):
            first, second = slots(batch, pair)
            nu = jnp.concatenate([nu_rows[first][:1], nu_rows[second][:1]], axis=1)
            nu4 = jnp.broadcast_to(4.0 * nu, (CHUNK, 2 * width))
            nu5 = jnp.broadcast_to(5.0 * nu, (CHUNK, 2 * width))
            for r in range(width // CHUNK):
                sq = jnp.maximum(ahead[pair, r * CHUNK : (r + 1) * CHUNK], TINY)
                base = jnp.maximum(nu4 - sq * lax.rsqrt(sq), 0.0)
                base2 = base * base
                term = (base2 * base2) * (nu5 - base)
                term = term[:, :width] + term[:, width:]
                sums[r] = term if sums[r] is None else sums[r] + term
        for pair in range(BATCH // 2):
            ahead[pair] = squares(later, pair)
        cell = cell_of[batch]
        for r in range(width // CHUNK):
            total[cell, r * CHUNK : (r + 1) * CHUNK] += sums[r]
        return carry

    lax.fori_loop(0, batches, step, 0)
    inv = jnp.concatenate([own_ref[cell][6:7] for cell in range(own)], axis=0)
    summed = jnp.concatenate(
        [jnp.sum(jnp.transpose(total[cell]), axis=0, keepdims=True) for cell in range(own)], axis=0
    )
    dens = (NORM / 256.0) * (inv * inv * inv) * summed
    density[...] = dens
    value = entropy[...] * jnp.exp(jnp.log(dens) * (-1.0 / 3.0))
    for copy in range(weight.shape[0]):
        weight[copy] = value


def pair_sums(sizes, index, counts, left, table, rows, total, ahead, cell_of, slot_of):
    own = sizes[3]
    width = table.shape[2]
    total[...] = jnp.zeros_like(total)
    batches = list_batches(own, counts, cell_of, slot_of)

    def slots(batch, pair):
        cell, slot = cell_of[batch], slot_of[batch] + 2 * pair
        return index[cell, slot], index[cell, slot + 1]

    def squares(batch, pair):
        first, second = slots(batch, pair)
        others = jnp.transpose(jnp.concatenate([table[first], table[second]], axis=0))
        return jnp.dot(others, left[cell_of[batch]], preferred_element_type=jnp.float32)

    for pair in range(BATCH // 2):
        ahead[pair] = squares(0, pair)

    def step(batch, carry):
        later = jnp.minimum(batch + 1, batches - 1)
        added = None
        for pair in range(BATCH // 2):
            highs, lows = [], []
            for r in range(width // CHUNK):
                sq = jnp.maximum(ahead[pair, r * CHUNK : (r + 1) * CHUNK], TINY)
                base = jnp.maximum(1.0 - sq * lax.rsqrt(sq), 0.0)
                cube = base * base * base
                high = cube.astype(jnp.bfloat16)
                highs.append(high)
                lows.append((cube - high.astype(jnp.float32)).astype(jnp.bfloat16))
            high = jnp.concatenate(highs, axis=0)
            low = jnp.concatenate(lows, axis=0)
            cubes = jnp.concatenate(
                [
                    jnp.concatenate([high[:, :width], high[:, width:]], axis=0),
                    jnp.concatenate([low[:, :width], low[:, width:]], axis=0),
                ],
                axis=1,
            )
            first, second = slots(batch, pair)
            both = jnp.concatenate([rows[first], rows[second]], axis=1)
            part = jnp.dot(both, cubes, preferred_element_type=jnp.float32)
            added = part if added is None else added + part
        for pair in range(BATCH // 2):
            ahead[pair] = squares(later, pair)
        total[cell_of[batch]] += added
        return carry

    lax.fori_loop(0, batches, step, 0)


def folded(total, width):
    both = total[:, :width] + total[:, width:]
    return both[:ROWS] + both[ROWS : 2 * ROWS] + both[2 * ROWS : 3 * ROWS]


def padded_parts(parts):
    pad = jnp.zeros((8 * ROWS - parts.shape[0], parts.shape[1]), parts.dtype)
    return jnp.concatenate([parts, pad], axis=0).astype(jnp.bfloat16)


def block_diagonal(parts):
    pad = jnp.zeros((8 * ROWS - parts.shape[0], parts.shape[1]), parts.dtype)
    whole = jnp.concatenate([parts, pad], axis=0)
    empty = jnp.zeros_like(whole)
    return jnp.concatenate(
        [
            jnp.concatenate([whole, empty], axis=1),
            jnp.concatenate([empty, whole], axis=1),
        ],
        axis=0,
    ).astype(jnp.bfloat16)


def own_kernel(sizes, index, counts, own_ref, *rest):
    refs, (out, other_table, other_rows, left, table, rows, total, ahead, cell_of, slot_of) = (
        rest[:-10],
        rest[-10:],
    )

    def fill(at, v, shift):
        placed = right_rows(v, shift)
        inv2 = v[6:7] * v[6:7]
        table[at] = padded_parts(right_parts(placed))
        rows[at] = sum_parts(v[5:6] * placed)
        other_table[at] = padded_parts(right_parts((0.25 * inv2) * placed))
        other_rows[at] = (v[5:6] * (inv2 * inv2 * v[6:7])) * placed

    table_cells(refs, sizes, fill)
    for cell in range(sizes[3]):
        v = own_ref[cell]
        left[cell] = block_diagonal(left_parts((0.25 * (v[6:7] * v[6:7])) * left_rows(v)))
    pair_sums(sizes, index, counts, left, table, rows, total, ahead, cell_of, slot_of)
    for cell in range(sizes[3]):
        out[cell] = folded(total[cell], own_ref.shape[2])


def other_kernel(
    sizes,
    index,
    counts,
    place,
    own_ref,
    weight_own,
    part,
    weight_all,
    table,
    other_rows,
    out,
    left,
    rows,
    total,
    ahead,
    cell_of,
    slot_of,
):
    groups, depth, cores, own = sizes
    for block in range(3 * cores):
        side, core = block // cores, block % cores
        group = lax.rem(place[0] + side - 1 + groups, groups)

        def fill(step, carry, block=block, core=core, group=group):
            z = lax.rem(place[1] + step, depth)
            source = (group * depth + z) * cores + lax.rem(place[2] + core, cores)
            for cell in range(own):
                at = (block * depth + step) * own + cell
                rows[at] = sum_parts(weight_all[source, cell : cell + 1] * other_rows[at])
            return carry

        lax.fori_loop(0, depth, fill, 0, unroll=2)
    for cell in range(own):
        left[cell] = block_diagonal(left_parts(left_rows(own_ref[cell])))
    pair_sums(sizes, index, counts, left, table, rows, total, ahead, cell_of, slot_of)
    for cell in range(own):
        v = own_ref[cell]
        inv2 = v[6:7] * v[6:7]
        scale = weight_own[0, cell : cell + 1] * (inv2 * inv2 * v[6:7])
        both = scale * part[cell] + folded(total[cell], own_ref.shape[2])
        for k in range(3):
            out[k, cell : cell + 1, :] = (5.0 * NORM) * (
                v[k : k + 1] * both[3:4] - both[k : k + 1]
            )


def call(kernel, out_shape, scratch, scalars, arrays):
    smem = pl.BlockSpec(memory_space=pltpu.SMEM)
    vmem = pl.BlockSpec(memory_space=pltpu.VMEM)
    many = isinstance(out_shape, tuple)
    return pl.pallas_call(
        kernel,
        out_shape=out_shape,
        in_specs=[smem] * len(scalars) + [vmem] * len(arrays),
        out_specs=(vmem,) * len(out_shape) if many else vmem,
        scratch_shapes=scratch,
        compiler_params=pltpu.CompilerParams(vmem_limit_bytes=VMEM_LIMIT),
        cost_estimate=pl.CostEstimate(
            flops=4_000_000_000, bytes_accessed=4_000_000, transcendentals=4_000_000
        ),
    )(*scalars, *arrays)


def on_device(particles, entropy, lists, counts):
    own, _, width = particles.shape
    groups, depth, cores = (lax.axis_size(a) for a in ("grp", "z", "core"))
    sizes = (groups, depth, cores, own)
    place = jnp.stack([lax.axis_index(a) for a in ("grp", "z", "core")]).astype(jnp.int32)

    rows = call(
        rows_kernel,
        jax.ShapeDtypeStruct((own, ROWS, width), jnp.float32),
        [],
        [],
        [jnp.transpose(particles, (1, 0, 2))],
    )

    def shifted(block, axis, by):
        count = lax.axis_size(axis)
        return lax.ppermute(block, axis, [(i, (i - by) % count) for i in range(count)])

    got = {0: rows}
    for by in range(1, depth):
        got[by] = shifted(rows, "z", by)
    column = jnp.concatenate([got[by] for by in range(depth)], axis=0)
    sides = [shifted(column, "grp", -1), column, shifted(column, "grp", 1)]
    refs = []
    for side in sides:
        refs.append(side)
        for by in range(1, cores):
            refs.append(shifted(side, "core", by))

    def table_index(cell_id):
        side = (cell_id // (depth * cores * own) - lax.axis_index("grp") + 1 + groups) % groups
        member = cell_id // own
        z = (member // cores - lax.axis_index("z") + depth) % depth
        core = (member - lax.axis_index("core") + cores) % cores
        return ((side * cores + core) * depth + z) * own + cell_id % own

    index = table_index(lists)
    cells = 3 * cores * depth * own
    shape = jax.ShapeDtypeStruct
    f32, bf16 = jnp.float32, jnp.bfloat16
    most = own * (lists.shape[1] // BATCH)
    order = [pltpu.SMEM((most,), jnp.int32), pltpu.SMEM((most,), jnp.int32)]
    ahead = pltpu.VMEM((BATCH // 2, width, 2 * width), f32)
    everyone = groups * depth * cores
    density, weight = call(
        functools.partial(density_kernel, sizes),
        (shape((own, width), f32), shape((everyone, own, width), f32)),
        [
            pltpu.VMEM((cells, 6 * ROWS, width), bf16),
            pltpu.VMEM((cells, ROWS, width), f32),
            pltpu.VMEM((own, width, 6 * ROWS), bf16),
            pltpu.VMEM((own, width, width), f32),
            ahead,
            *order,
        ],
        [index, counts],
        [rows, entropy, *refs],
    )
    weight_all = lax.all_to_all(weight, ("grp", "z", "core"), 0, 0, tiled=True)
    left = pltpu.VMEM((own, 16 * ROWS, 2 * width), bf16)
    table = (cells, 8 * ROWS, width)
    sums = pltpu.VMEM((cells, 4 * ROWS, width), bf16)
    total = pltpu.VMEM((own, 4 * ROWS, 2 * width), f32)
    part, other_table, other_rows = call(
        functools.partial(own_kernel, sizes),
        (shape((own, ROWS, width), f32), shape(table, bf16), shape((cells, ROWS, width), f32)),
        [left, pltpu.VMEM(table, bf16), sums, total, ahead, *order],
        [index, counts],
        [rows, *refs],
    )
    accel = call(
        functools.partial(other_kernel, sizes),
        shape((3, own, width), f32),
        [left, sums, total, ahead, *order],
        [index, counts, place],
        [rows, weight, part, weight_all, other_table, other_rows],
    )
    return density, jnp.transpose(accel, (1, 0, 2))


def solution(mesh):
    groups, members = mesh.devices.shape
    cores = 2 if members % 2 == 0 else 1
    split = Mesh(mesh.devices.reshape(groups, members // cores, cores), ("grp", "z", "core"))
    cells = ("grp", "z", "core")
    return jax.shard_map(
        on_device,
        mesh=split,
        in_specs=(P(cells, None, None), P(cells, None), P(cells, None), P(cells)),
        out_specs=(P(cells, None), P(cells, None, None)),
        check_vma=False,
    )
```

profile of v0, /device:TPU:15, one launch (start us, length us, event | category | flops | bytes accessed | tf_op | source)
XLA Modules:
  0.0 47.9 jit_solution(7453480022618116024)
XLA Ops:
  0.6 0.0 copy-start
  0.6 0.7 %copy-done = f32[4,5,128]{2,0,1:T(4,128)S(1)} copy-done((f32[4,5,128]{2,0,1:T(4,128)S(1)}, f32[4,5,128]{2,0,1:T(4,128)}, u32[]{:S(2)}) %copy-start) | copy-done | bytes 10264
  1.4 1.3 %collective-permute-start.2 = (f32[4,8,128]{2,1,0:T(8,128)S(1)}, f32[4,8,128]{2,1,0:T(8,128)S(1)}, u32[]{:S(2)}, u32[]{:S(2)}) collective-permute-start(f32[4,8,128]{2,1,0:T(8,128)S(1)} %shard_map.59.own_ref), channel_id=1, source_target_pairs={{0,2},{2,4},{4,6},{6,0},{1,3},{3,5},{5,7},{7,1},{8,10},{10,12},{12... | collective-permute-start | bytes 49160 | tf_op jit(solution)/shard_map/ppermute | solution.py:336
  2.7 1.1 %collective-permute-start.1 = (f32[4,8,128]{2,1,0:T(8,128)S(1)}, f32[4,8,128]{2,1,0:T(8,128)S(1)}, u32[]{:S(2)}, u32[]{:S(2)}) collective-permute-start(f32[4,8,128]{2,1,0:T(8,128)S(1)} %shard_map.59.own_ref), channel_id=1, source_target_pairs={{0,4},{2,6},{4,0},{6,2},{1,5},{3,7},{5,1},{7,3},{8,12},{10,14},{12... | collective-permute-start | bytes 49160 | tf_op jit(solution)/shard_map/ppermute | solution.py:336
  3.8 1.4 %collective-permute-start = (f32[4,8,128]{2,1,0:T(8,128)S(1)}, f32[4,8,128]{2,1,0:T(8,128)S(1)}, u32[]{:S(2)}, u32[]{:S(2)}) collective-permute-start(f32[4,8,128]{2,1,0:T(8,128)S(1)} %shard_map.59.own_ref), channel_id=1, source_target_pairs={{0,6},{2,0},{4,2},{6,4},{1,7},{3,1},{5,3},{7,5},{8,14},{10,8},{12,... | collective-permute-start | bytes 49160 | tf_op jit(solution)/shard_map/ppermute | solution.py:336
  5.2 0.0 collective-permute-done.2
  5.2 1.0 %collective-permute-done.1 = f32[4,8,128]{2,1,0:T(8,128)S(1)} collective-permute-done((f32[4,8,128]{2,1,0:T(8,128)S(1)}, f32[4,8,128]{2,1,0:T(8,128)S(1)}, u32[]{:S(2)}, u32[]{:S(2)}) %collective-permute-start.1) | collective-permute-done | bytes 16416 | tf_op jit(solution)/shard_map/ppermute | solution.py:336
  6.2 0.2 collective-permute-done
  6.4 0.2 collective-permute-start.3
  6.6 1.3 %collective-permute-start.6 = (f32[16,8,128]{2,1,0:T(8,128)S(1)}, f32[16,8,128]{2,1,0:T(8,128)S(1)}, u32[]{:S(2)}, u32[]{:S(2)}) collective-permute-start(f32[16,8,128]{2,1,0:T(8,128)S(1)} %pad_maximum_fusion.rest_2_), channel_id=1, source_target_pairs={{0,24},{8,0},{16,8},{24,16},{1,25},{9,1},{17,9},{25,17},{2,26},{10... | collective-permute-start | bytes 196616 | tf_op jit(solution)/shard_map/ppermute | solution.py:336
  7.9 2.9 %collective-permute-start.5 = (f32[16,8,128]{2,1,0:T(8,128)S(1)}, f32[16,8,128]{2,1,0:T(8,128)S(1)}, u32[]{:S(2)}, u32[]{:S(2)}) collective-permute-start(f32[16,8,128]{2,1,0:T(8,128)S(1)} %pad_maximum_fusion.rest_2_), channel_id=1, source_target_pairs={{0,1},{1,0},{2,3},{3,2},{4,5},{5,4},{6,7},{7,6},{8,9},{9,8},{10,11... | collective-permute-start | bytes 196616 | tf_op jit(solution)/shard_map/ppermute | solution.py:336
  10.8 0.0 collective-permute-done.3.rest_0_
  10.8 2.1 %collective-permute-start.4 = (f32[16,8,128]{2,1,0:T(8,128)S(1)}, f32[16,8,128]{2,1,0:T(8,128)S(1)}, u32[]{:S(2)}, u32[]{:S(2)}) collective-permute-start(f32[16,8,128]{2,1,0:T(8,128)S(1)} %collective-permute-done.3.rest_0_), channel_id=1, source_target_pairs={{0,1},{1,0},{2,3},{3,2},{4,5},{5,4},{6,7},{7,6},{8,9},{9,8},{10,11... | collective-permute-start | bytes 196616 | tf_op jit(solution)/shard_map/ppermute | solution.py:336
  12.9 0.0 collective-permute-done.6.rest_4_
  12.9 1.2 %collective-permute-start.7 = (f32[16,8,128]{2,1,0:T(8,128)S(1)}, f32[16,8,128]{2,1,0:T(8,128)S(1)}, u32[]{:S(2)}, u32[]{:S(2)}) collective-permute-start(f32[16,8,128]{2,1,0:T(8,128)S(1)} %collective-permute-done.6.rest_4_), channel_id=1, source_target_pairs={{0,1},{1,0},{2,3},{3,2},{4,5},{5,4},{6,7},{7,6},{8,9},{9,8},{10,11... | collective-permute-start | bytes 196616 | tf_op jit(solution)/shard_map/ppermute | solution.py:336
  14.1 0.1 pad_add_fusion.place
  14.2 0.0 collective-permute-done.5.rest_3_
  14.2 0.0 collective-permute-done.4.rest_1_
  14.2 0.8 %collective-permute-done.7.rest_5_ = f32[16,8,128]{2,1,0:T(8,128)S(1)} collective-permute-done((f32[16,8,128]{2,1,0:T(8,128)S(1)}, f32[16,8,128]{2,1,0:T(8,128)S(1)}, u32[]{:S(2)}, u32[]{:S(2)}) %collective-permute-start.7) | collective-permute-done | bytes 65568 | tf_op jit(solution)/shard_map/ppermute | solution.py:336
  15.1 8.9 %shard_map.60 = (f32[4,128]{1,0:T(4,128)}, f32[32,4,128]{2,1,0:T(4,128)}) custom-call(s32[4,64]{1,0:T(4,128)S(1)} %fusion.9.index, s32[4]{0:T(128)S(1)} %copy-done.2, f32[4,8,128]{2,1,0:T(8,128)S(1)} %shard_map.59.own_ref, f32[4,128]{1,0:T(4,128)S(1)} %copy-done.1, f32[16,8,128]{2,1,0:T(8,128)S(1)} %collective-permute-done.3.rest_0_, ...), custom_call_target="tpu_custom_call" | custom-call | flops 4000000000 | bytes 4000000 | tf_op jit(solution)/shard_map/pallas_call | solution.py:307
  23.9 6.5 %all-to-all-start = ((f32[32,4,128]{2,1,0:T(4,128)}), f32[32,4,128]{2,1,0:T(4,128)S(1)}, u32[]{:S(2)}, u32[]{:S(2)}) async-start(f32[32,4,128]{2,1,0:T(4,128)} %get-tuple-element.8.weight_own), calls=%async_computation | async-start | bytes 131072 | tf_op jit(solution)/shard_map/all_to_all | solution.py:378
  30.5 8.4 %shard_map.61 = (f32[4,8,128]{2,1,0:T(8,128)S(1)}, bf16[96,64,128]{2,1,0:T(8,128)(2,1)S(1)}, f32[96,8,128]{2,1,0:T(8,128)S(1)}) custom-call(s32[4,64]{1,0:T(4,128)S(1)} %fusion.9.index, s32[4]{0:T(128)S(1)} %copy-done.2, f32[4,8,128]{2,1,0:T(8,128)S(1)} %shard_map.59.own_ref, f32[16,8,128]{2,1,0:T(8,128)S(1)} %collective-permute-done.3.rest_0_, ...), custom_call_target="tpu_custom_call" | custom-call | flops 4000000000 | bytes 4000000 | tf_op jit(solution)/shard_map/pallas_call | solution.py:307
  38.9 0.0 all-to-all-done.weight_all
  38.9 9.0 %shard_map.62 = f32[3,4,128]{2,1,0:T(4,128)} custom-call(s32[4,64]{1,0:T(4,128)S(1)} %fusion.9.index, s32[4]{0:T(128)S(1)} %copy-done.2, s32[3]{0:T(128)S(1)} %pad_add_fusion.place, f32[4,8,128]{2,1,0:T(8,128)S(1)} %shard_map.59.own_ref, f32[32,4,128]{2,1,0:T(4,128)} %get-tuple-element.8.weight_own, f32[4,8,128]{2,1,0:T(8,128)S(1)} %get-tuple-element.9.part, ...), custom_call_target="tpu_custom_call" | custom-call | flops 4000000000 | bytes 4000000 | tf_op jit(solution)/shard_map/pallas_call | solution.py:307
  (9 shorter events, 0.1 us)
Async XLA Ops:
  0.6 0.7 %copy-start = (f32[4,5,128]{2,0,1:T(4,128)S(1)}, f32[4,5,128]{2,0,1:T(4,128)}, u32[]{:S(2)}) copy-start(f32[4,5,128]{2,0,1:T(4,128)} %param.4) | copy-start | bytes 30724
  1.3 6.5 %copy-start.3 = (s32[4,64]{1,0:T(4,128)S(1)}, s32[4,64]{1,0:T(4,128)}, u32[]{:S(2)}) copy-start(s32[4,64]{1,0:T(4,128)} %param.6) | copy-start | bytes 3076
  1.3 13.7 %copy-start.1 = (f32[4,128]{1,0:T(4,128)S(1)}, f32[4,128]{1,0:T(4,128)}, u32[]{:S(2)}) copy-start(f32[4,128]{1,0:T(4,128)} %entropy.1) | copy-start | bytes 6148
  1.3 13.7 %copy-start.2 = (s32[4]{0:T(128)S(1)}, s32[4]{0:T(128)}, u32[]{:S(2)}) copy-start(s32[4]{0:T(128)} %counts.5) | copy-start | bytes 52
  1.4 3.8 %collective-permute-start.2 = (f32[4,8,128]{2,1,0:T(8,128)S(1)}, f32[4,8,128]{2,1,0:T(8,128)S(1)}, u32[]{:S(2)}, u32[]{:S(2)}) collective-permute-start(f32[4,8,128]{2,1,0:T(8,128)S(1)} %shard_map.59.own_ref), channel_id=1, source_target_pairs={{0,2},{2,4},{4,6},{6,0},{1,3},{3,5},{5,7},{7,1},{8,10},{10,12},{12... | collective-permute-start | bytes 49160 | tf_op jit(solution)/shard_map/ppermute | solution.py:336
  2.7 3.5 %collective-permute-start.1 = (f32[4,8,128]{2,1,0:T(8,128)S(1)}, f32[4,8,128]{2,1,0:T(8,128)S(1)}, u32[]{:S(2)}, u32[]{:S(2)}) collective-permute-start(f32[4,8,128]{2,1,0:T(8,128)S(1)} %shard_map.59.own_ref), channel_id=1, source_target_pairs={{0,4},{2,6},{4,0},{6,2},{1,5},{3,7},{5,1},{7,3},{8,12},{10,14},{12... | collective-permute-start | bytes 49160 | tf_op jit(solution)/shard_map/ppermute | solution.py:336
  3.8 2.6 %collective-permute-start = (f32[4,8,128]{2,1,0:T(8,128)S(1)}, f32[4,8,128]{2,1,0:T(8,128)S(1)}, u32[]{:S(2)}, u32[]{:S(2)}) collective-permute-start(f32[4,8,128]{2,1,0:T(8,128)S(1)} %shard_map.59.own_ref), channel_id=1, source_target_pairs={{0,6},{2,0},{4,2},{6,4},{1,7},{3,1},{5,3},{7,5},{8,14},{10,8},{12,... | collective-permute-start | bytes 49160 | tf_op jit(solution)/shard_map/ppermute | solution.py:336
  6.4 4.4 %collective-permute-start.3 = (f32[16,8,128]{2,1,0:T(8,128)S(1)}, f32[16,8,128]{2,1,0:T(8,128)S(1)}, u32[]{:S(2)}, u32[]{:S(2)}) collective-permute-start(f32[16,8,128]{2,1,0:T(8,128)S(1)} %pad_maximum_fusion.rest_2_), channel_id=1, source_target_pairs={{0,8},{8,16},{16,24},{24,0},{1,9},{9,17},{17,25},{25,1},{2,10},{10... | collective-permute-start | bytes 196616 | tf_op jit(solution)/shard_map/ppermute | solution.py:336
  6.6 6.3 %collective-permute-start.6 = (f32[16,8,128]{2,1,0:T(8,128)S(1)}, f32[16,8,128]{2,1,0:T(8,128)S(1)}, u32[]{:S(2)}, u32[]{:S(2)}) collective-permute-start(f32[16,8,128]{2,1,0:T(8,128)S(1)} %pad_maximum_fusion.rest_2_), channel_id=1, source_target_pairs={{0,24},{8,0},{16,8},{24,16},{1,25},{9,1},{17,9},{25,17},{2,26},{10... | collective-permute-start | bytes 196616 | tf_op jit(solution)/shard_map/ppermute | solution.py:336
  7.9 6.3 %collective-permute-start.5 = (f32[16,8,128]{2,1,0:T(8,128)S(1)}, f32[16,8,128]{2,1,0:T(8,128)S(1)}, u32[]{:S(2)}, u32[]{:S(2)}) collective-permute-start(f32[16,8,128]{2,1,0:T(8,128)S(1)} %pad_maximum_fusion.rest_2_), channel_id=1, source_target_pairs={{0,1},{1,0},{2,3},{3,2},{4,5},{5,4},{6,7},{7,6},{8,9},{9,8},{10,11... | collective-permute-start | bytes 196616 | tf_op jit(solution)/shard_map/ppermute | solution.py:336
  10.8 3.5 %collective-permute-start.4 = (f32[16,8,128]{2,1,0:T(8,128)S(1)}, f32[16,8,128]{2,1,0:T(8,128)S(1)}, u32[]{:S(2)}, u32[]{:S(2)}) collective-permute-start(f32[16,8,128]{2,1,0:T(8,128)S(1)} %collective-permute-done.3.rest_0_), channel_id=1, source_target_pairs={{0,1},{1,0},{2,3},{3,2},{4,5},{5,4},{6,7},{7,6},{8,9},{9,8},{10,11... | collective-permute-start | bytes 196616 | tf_op jit(solution)/shard_map/ppermute | solution.py:336
  12.9 2.1 %collective-permute-start.7 = (f32[16,8,128]{2,1,0:T(8,128)S(1)}, f32[16,8,128]{2,1,0:T(8,128)S(1)}, u32[]{:S(2)}, u32[]{:S(2)}) collective-permute-start(f32[16,8,128]{2,1,0:T(8,128)S(1)} %collective-permute-done.6.rest_4_), channel_id=1, source_target_pairs={{0,1},{1,0},{2,3},{3,2},{4,5},{5,4},{6,7},{7,6},{8,9},{9,8},{10,11... | collective-permute-start | bytes 196616 | tf_op jit(solution)/shard_map/ppermute | solution.py:336
  23.9 15.0 %all-to-all-start = ((f32[32,4,128]{2,1,0:T(4,128)}), f32[32,4,128]{2,1,0:T(4,128)S(1)}, u32[]{:S(2)}, u32[]{:S(2)}) async-start(f32[32,4,128]{2,1,0:T(4,128)} %get-tuple-element.8.weight_own), calls=%async_computation | async-start | bytes 131072 | tf_op jit(solution)/shard_map/all_to_all | solution.py:378
where the time goes:
time: 48.2 us; the launch traced here: 47.9 us
  Pallas kernels  26.3 us (55%)
  starting transfers between devices  18.1 us (38%)
  waiting for transfers between devices  2.03 us (4%)
  local copies, waits for them, and re-layouts  0.71 us (1%)
  between operations  0.68 us (1%)
    pallas_call x4, Pallas kernels, call(): pl.pallas_call(kernel, out_shape=out_shape, in_specs=[smem] * len(scalars...  26.3 us
    ppermute x8, starting transfers between devices, shifted(): lax.ppermute(block, axis, [(i, (i - by) % count) for i in range(count)])  11.5 us
    all_to_all x1, starting transfers between devices, on_device(): weight_all = lax.all_to_all(weight, ('grp', 'z', 'core'), 0, 0, tiled=True)  6.55 us
    ppermute x8, waiting for transfers between devices, shifted(): lax.ppermute(block, axis, [(i, (i - by) % count) for i in range(count)])  2.03 us
  transfers between devices with their start and end apart: 9, of which 3 were waited for; matrix products, arithmetic and copies ran while one was open for 0% of the time, Pallas kernels for 18%

commit v1 on v0

--- a/solution.py
+++ b/solution.py
@@ -100,7 +100,9 @@
     def fill(at, v, shift):
         nu = v[7:8]
         table[at] = right_parts((nu * nu) * right_rows(v, shift)).astype(jnp.bfloat16)
-        nu_rows[at] = jnp.broadcast_to(nu, v.shape)
+        nu_rows[at] = jnp.concatenate(
+            [jnp.broadcast_to(4.0 * nu, v.shape), jnp.broadcast_to(5.0 * nu, v.shape)], axis=0
+        )
 
     table_cells(refs, sizes, fill)
     for cell in range(own):
@@ -114,37 +116,53 @@
         cell, slot = cell_of[batch], slot_of[batch] + 2 * pair
         return index[cell, slot], index[cell, slot + 1]
 
-    def squares(batch, pair):
+    pairs = BATCH // 2
+
+    def fill_pair(batch, half, pair):
         first, second = slots(batch, pair)
         right = jnp.concatenate([table[first], table[second]], axis=1)
-        return jnp.dot(left[cell_of[batch]], right, preferred_element_type=jnp.float32)
-
-    for pair in range(BATCH // 2):
-        ahead[pair] = squares(0, pair)
-
-    def step(batch, carry):
-        later = jnp.minimum(batch + 1, batches - 1)
+        ahead[half, pair] = jnp.dot(
+            left[cell_of[batch]], right, preferred_element_type=jnp.float32
+        )
+
+    def fill(batch, half):
+        for pair in range(pairs):
+            fill_pair(batch, half, pair)
+
+    def add(batch, half, later=None):
         sums = [None] * (width // CHUNK)
-        for pair in range(BATCH // 2):
+        if later is not None:
+            fill(later, 1 - half)
+        for pair in range(pairs):
             first, second = slots(batch, pair)
-            nu = jnp.concatenate([nu_rows[first][:1], nu_rows[second][:1]], axis=1)
-            nu4 = jnp.broadcast_to(4.0 * nu, (CHUNK, 2 * width))
-            nu5 = jnp.broadcast_to(5.0 * nu, (CHUNK, 2 * width))
+            nu = jnp.concatenate([nu_rows[first], nu_rows[second]], axis=1)
+            nu4 = jnp.concatenate([nu[:ROWS]] * (CHUNK // ROWS), axis=0)
+            nu5 = jnp.concatenate([nu[ROWS:]] * (CHUNK // ROWS), axis=0)
             for r in range(width // CHUNK):
-                sq = jnp.maximum(ahead[pair, r * CHUNK : (r + 1) * CHUNK], TINY)
+                sq = jnp.maximum(ahead[half, pair, r * CHUNK : (r + 1) * CHUNK], TINY)
                 base = jnp.maximum(nu4 - sq * lax.rsqrt(sq), 0.0)
                 base2 = base * base
                 term = (base2 * base2) * (nu5 - base)
                 term = term[:, :width] + term[:, width:]
                 sums[r] = term if sums[r] is None else sums[r] + term
-        for pair in range(BATCH // 2):
-            ahead[pair] = squares(later, pair)
         cell = cell_of[batch]
         for r in range(width // CHUNK):
             total[cell, r * CHUNK : (r + 1) * CHUNK] += sums[r]
+
+    last = batches - 1
+    fill(0, 0)
+
+    def step(k, carry):
+        add(2 * k, 0, 2 * k + 1)
+        add(2 * k + 1, 1, jnp.minimum(2 * k + 2, last))
         return carry
 
-    lax.fori_loop(0, batches, step, 0)
+    lax.fori_loop(0, lax.div(batches, 2), step, 0)
+
+    @pl.when(lax.rem(batches, 2) == 1)
+    def _():
+        add(last, 0)
+
     inv = jnp.concatenate([own_ref[cell][6:7] for cell in range(own)], axis=0)
     summed = jnp.concatenate(
         [jnp.sum(jnp.transpose(total[cell]), axis=0, keepdims=True) for cell in range(own)], axis=0
@@ -159,6 +177,7 @@
 def pair_sums(sizes, index, counts, left, table, rows, total, ahead, cell_of, slot_of):
     own = sizes[3]
     width = table.shape[2]
+    pairs = BATCH // 2
     total[...] = jnp.zeros_like(total)
     batches = list_batches(own, counts, cell_of, slot_of)
 
@@ -166,21 +185,25 @@
         cell, slot = cell_of[batch], slot_of[batch] + 2 * pair
         return index[cell, slot], index[cell, slot + 1]
 
-    def squares(batch, pair):
-        first, second = slots(batch, pair)
-        others = jnp.transpose(jnp.concatenate([table[first], table[second]], axis=0))
-        return jnp.dot(others, left[cell_of[batch]], preferred_element_type=jnp.float32)
-
-    for pair in range(BATCH // 2):
-        ahead[pair] = squares(0, pair)
-
-    def step(batch, carry):
-        later = jnp.minimum(batch + 1, batches - 1)
+    def fill(batch, half):
+        others = []
+        for pair in range(pairs):
+            first, second = slots(batch, pair)
+            others.append(jnp.transpose(jnp.concatenate([table[first], table[second]], axis=0)))
+        ahead[half] = jnp.dot(
+            jnp.concatenate(others, axis=0),
+            left[cell_of[batch]],
+            preferred_element_type=jnp.float32,
+        )
+
+    def add(batch, half, later=None):
         added = None
-        for pair in range(BATCH // 2):
+        if later is not None:
+            fill(later, 1 - half)
+        for pair in range(pairs):
             highs, lows = [], []
-            for r in range(width // CHUNK):
-                sq = jnp.maximum(ahead[pair, r * CHUNK : (r + 1) * CHUNK], TINY)
+            for r in range(pair * width, (pair + 1) * width, CHUNK):
+                sq = jnp.maximum(ahead[half, r : r + CHUNK], TINY)
                 base = jnp.maximum(1.0 - sq * lax.rsqrt(sq), 0.0)
                 cube = base * base * base
                 high = cube.astype(jnp.bfloat16)
@@ -199,12 +222,21 @@
             both = jnp.concatenate([rows[first], rows[second]], axis=1)
             part = jnp.dot(both, cubes, preferred_element_type=jnp.float32)
             added = part if added is None else added + part
-        for pair in range(BATCH // 2):
-            ahead[pair] = squares(later, pair)
         total[cell_of[batch]] += added
+
+    last = batches - 1
+    fill(0, 0)
+
+    def step(k, carry):
+        add(2 * k, 0, 2 * k + 1)
+        add(2 * k + 1, 1, jnp.minimum(2 * k + 2, last))
         return carry
 
-    lax.fori_loop(0, batches, step, 0)
+    lax.fori_loop(0, lax.div(batches, 2), step, 0)
+
+    @pl.when(lax.rem(batches, 2) == 1)
+    def _():
+        add(last, 0)
 
 
 def folded(total, width):
@@ -359,14 +391,14 @@
     f32, bf16 = jnp.float32, jnp.bfloat16
     most = own * (lists.shape[1] // BATCH)
     order = [pltpu.SMEM((most,), jnp.int32), pltpu.SMEM((most,), jnp.int32)]
-    ahead = pltpu.VMEM((BATCH // 2, width, 2 * width), f32)
+    ahead = pltpu.VMEM((2, BATCH // 2, width, 2 * width), f32)
     everyone = groups * depth * cores
     density, weight = call(
         functools.partial(density_kernel, sizes),
         (shape((own, width), f32), shape((everyone, own, width), f32)),
         [
             pltpu.VMEM((cells, 6 * ROWS, width), bf16),
-            pltpu.VMEM((cells, ROWS, width), f32),
+            pltpu.VMEM((cells, 2 * ROWS, width), f32),
             pltpu.VMEM((own, width, 6 * ROWS), bf16),
             pltpu.VMEM((own, width, width), f32),
             ahead,
@@ -376,6 +408,7 @@
         [rows, entropy, *refs],
     )
     weight_all = lax.all_to_all(weight, ("grp", "z", "core"), 0, 0, tiled=True)
+    ahead = pltpu.VMEM((2, BATCH // 2 * width, 2 * width), f32)
     left = pltpu.VMEM((own, 16 * ROWS, 2 * width), bf16)
     table = (cells, 8 * ROWS, width)
     sums = pltpu.VMEM((cells, 4 * ROWS, width), bf16)

time: 48.2 us -> 46.2 us (0.959)
  the two profiles are of different devices: /device:TPU:15 before, /device:TPU:0 now
where the time goes in v1:
time: 46.2 us; the launch traced here: 45.7 us
  Pallas kernels  20.6 us (45%)
  starting transfers between devices  16.1 us (35%)
  waiting for transfers between devices  7.46 us (16%)
  local copies, waits for them, and re-layouts  0.71 us (2%)
  between operations  0.68 us (1%)
    pallas_call x4, Pallas kernels, call(): pl.pallas_call(kernel, out_shape=out_shape, in_specs=[smem] * len(scalars...  20.6 us
    ppermute x8, starting transfers between devices, shifted(): lax.ppermute(block, axis, [(i, (i - by) % count) for i in range(count)])  10 us
    ppermute x8, waiting for transfers between devices, shifted(): lax.ppermute(block, axis, [(i, (i - by) % count) for i in range(count)])  6.45 us
    all_to_all x1, starting transfers between devices, on_device(): weight_all = lax.all_to_all(weight, ('grp', 'z', 'core'), 0, 0, tiled=True)  6.1 us
    all_to_all x1, waiting for transfers between devices, on_device(): weight_all = lax.all_to_all(weight, ('grp', 'z', 'core'), 0, 0, tiled=True)  1.01 us
  transfers between devices with their start and end apart: 9, of which 7 were waited for; matrix products, arithmetic and copies ran while one was open for 0% of the time, Pallas kernels for 14%

profile of v1, /device:TPU:0, one launch (start us, length us, event | category | flops | bytes accessed | tf_op | source)
XLA Modules:
  0.0 45.7 jit_solution(6391181456024412770)
XLA Ops:
  0.6 0.7 %copy-done = f32[4,5,128]{2,0,1:T(4,128)S(1)} copy-done((f32[4,5,128]{2,0,1:T(4,128)S(1)}, f32[4,5,128]{2,0,1:T(4,128)}, u32[]{:S(2)}) %copy-start) | copy-done | bytes 10264
  1.4 3.1 %collective-permute-start.2 = (f32[4,8,128]{2,1,0:T(8,128)S(1)}, f32[4,8,128]{2,1,0:T(8,128)S(1)}, u32[]{:S(2)}, u32[]{:S(2)}) collective-permute-start(f32[4,8,128]{2,1,0:T(8,128)S(1)} %shard_map.59.own_ref), channel_id=1, source_target_pairs={{0,2},{2,4},{4,6},{6,0},{1,3},{3,5},{5,7},{7,1},{8,10},{10,12},{12... | collective-permute-start | bytes 49160 | tf_op jit(solution)/shard_map/ppermute | solution.py:368
  4.5 2.6 %collective-permute-start.1 = (f32[4,8,128]{2,1,0:T(8,128)S(1)}, f32[4,8,128]{2,1,0:T(8,128)S(1)}, u32[]{:S(2)}, u32[]{:S(2)}) collective-permute-start(f32[4,8,128]{2,1,0:T(8,128)S(1)} %shard_map.59.own_ref), channel_id=1, source_target_pairs={{0,4},{2,6},{4,0},{6,2},{1,5},{3,7},{5,1},{7,3},{8,12},{10,14},{12... | collective-permute-start | bytes 49160 | tf_op jit(solution)/shard_map/ppermute | solution.py:368
  7.1 1.3 %collective-permute-start = (f32[4,8,128]{2,1,0:T(8,128)S(1)}, f32[4,8,128]{2,1,0:T(8,128)S(1)}, u32[]{:S(2)}, u32[]{:S(2)}) collective-permute-start(f32[4,8,128]{2,1,0:T(8,128)S(1)} %shard_map.59.own_ref), channel_id=1, source_target_pairs={{0,6},{2,0},{4,2},{6,4},{1,7},{3,1},{5,3},{7,5},{8,14},{10,8},{12,... | collective-permute-start | bytes 49160 | tf_op jit(solution)/shard_map/ppermute | solution.py:368
  8.4 0.0 collective-permute-done.2
  8.4 0.8 %collective-permute-done.1 = f32[4,8,128]{2,1,0:T(8,128)S(1)} collective-permute-done((f32[4,8,128]{2,1,0:T(8,128)S(1)}, f32[4,8,128]{2,1,0:T(8,128)S(1)}, u32[]{:S(2)}, u32[]{:S(2)}) %collective-permute-start.1) | collective-permute-done | bytes 16416 | tf_op jit(solution)/shard_map/ppermute | solution.py:368
  9.2 1.6 %collective-permute-done = f32[4,8,128]{2,1,0:T(8,128)S(1)} collective-permute-done((f32[4,8,128]{2,1,0:T(8,128)S(1)}, f32[4,8,128]{2,1,0:T(8,128)S(1)}, u32[]{:S(2)}, u32[]{:S(2)}) %collective-permute-start) | collective-permute-done | bytes 16416 | tf_op jit(solution)/shard_map/ppermute | solution.py:368
  10.8 1.5 %collective-permute-start.3 = (f32[16,8,128]{2,1,0:T(8,128)S(1)}, f32[16,8,128]{2,1,0:T(8,128)S(1)}, u32[]{:S(2)}, u32[]{:S(2)}) collective-permute-start(f32[16,8,128]{2,1,0:T(8,128)S(1)} %pad_maximum_fusion.rest_2_), channel_id=1, source_target_pairs={{0,8},{8,16},{16,24},{24,0},{1,9},{9,17},{17,25},{25,1},{2,10},{10... | collective-permute-start | bytes 196616 | tf_op jit(solution)/shard_map/ppermute | solution.py:368
  12.3 1.4 %collective-permute-start.6 = (f32[16,8,128]{2,1,0:T(8,128)S(1)}, f32[16,8,128]{2,1,0:T(8,128)S(1)}, u32[]{:S(2)}, u32[]{:S(2)}) collective-permute-start(f32[16,8,128]{2,1,0:T(8,128)S(1)} %pad_maximum_fusion.rest_2_), channel_id=1, source_target_pairs={{0,24},{8,0},{16,8},{24,16},{1,25},{9,1},{17,9},{25,17},{2,26},{10... | collective-permute-start | bytes 196616 | tf_op jit(solution)/shard_map/ppermute | solution.py:368
  13.7 0.0 copy-done.3
  13.8 0.1 collective-permute-start.5
  13.8 2.1 %collective-permute-done.3.rest_0_ = f32[16,8,128]{2,1,0:T(8,128)S(1)} collective-permute-done((f32[16,8,128]{2,1,0:T(8,128)S(1)}, f32[16,8,128]{2,1,0:T(8,128)S(1)}, u32[]{:S(2)}, u32[]{:S(2)}) %collective-permute-start.3) | collective-permute-done | bytes 65568 | tf_op jit(solution)/shard_map/ppermute | solution.py:368
  16.0 0.0 collective-permute-start.4
  16.0 0.8 %collective-permute-done.6.rest_4_ = f32[16,8,128]{2,1,0:T(8,128)S(1)} collective-permute-done((f32[16,8,128]{2,1,0:T(8,128)S(1)}, f32[16,8,128]{2,1,0:T(8,128)S(1)}, u32[]{:S(2)}, u32[]{:S(2)}) %collective-permute-start.6) | collective-permute-done | bytes 65568 | tf_op jit(solution)/shard_map/ppermute | solution.py:368
  16.7 0.0 collective-permute-start.7
  16.7 0.1 pad_add_fusion.place
  16.8 0.0 collective-permute-done.5.rest_3_
  16.8 0.4 collective-permute-done.4.rest_1_
  17.2 0.8 %collective-permute-done.7.rest_5_ = f32[16,8,128]{2,1,0:T(8,128)S(1)} collective-permute-done((f32[16,8,128]{2,1,0:T(8,128)S(1)}, f32[16,8,128]{2,1,0:T(8,128)S(1)}, u32[]{:S(2)}, u32[]{:S(2)}) %collective-permute-start.7) | collective-permute-done | bytes 65568 | tf_op jit(solution)/shard_map/ppermute | solution.py:368
  18.0 7.2 %shard_map.60 = (f32[4,128]{1,0:T(4,128)}, f32[32,4,128]{2,1,0:T(4,128)}) custom-call(s32[4,64]{1,0:T(4,128)S(1)} %fusion.9.index, s32[4]{0:T(128)S(1)} %copy-done.2, f32[4,8,128]{2,1,0:T(8,128)S(1)} %shard_map.59.own_ref, f32[4,128]{1,0:T(4,128)S(1)} %copy-done.1, f32[16,8,128]{2,1,0:T(8,128)S(1)} %collective-permute-done.3.rest_0_, ...), custom_call_target="tpu_custom_call" | custom-call | flops 4000000000 | bytes 4000000 | tf_op jit(solution)/shard_map/pallas_call | solution.py:339
  25.2 6.1 %all-to-all-start = ((f32[32,4,128]{2,1,0:T(4,128)}), f32[32,4,128]{2,1,0:T(4,128)S(1)}, u32[]{:S(2)}, u32[]{:S(2)}) async-start(f32[32,4,128]{2,1,0:T(4,128)} %get-tuple-element.8.weight_own), calls=%async_computation | async-start | bytes 131072 | tf_op jit(solution)/shard_map/all_to_all | solution.py:410
  31.3 6.4 %shard_map.61 = (f32[4,8,128]{2,1,0:T(8,128)S(1)}, bf16[96,64,128]{2,1,0:T(8,128)(2,1)S(1)}, f32[96,8,128]{2,1,0:T(8,128)S(1)}) custom-call(s32[4,64]{1,0:T(4,128)S(1)} %fusion.9.index, s32[4]{0:T(128)S(1)} %copy-done.2, f32[4,8,128]{2,1,0:T(8,128)S(1)} %shard_map.59.own_ref, f32[16,8,128]{2,1,0:T(8,128)S(1)} %collective-permute-done.3.rest_0_, ...), custom_call_target="tpu_custom_call" | custom-call | flops 4000000000 | bytes 4000000 | tf_op jit(solution)/shard_map/pallas_call | solution.py:339
  37.7 1.0 %all-to-all-done.weight_all = f32[32,4,128]{2,1,0:T(4,128)S(1)} async-done(((f32[32,4,128]{2,1,0:T(4,128)}), f32[32,4,128]{2,1,0:T(4,128)S(1)}, u32[]{:S(2)}, u32[]{:S(2)}) %all-to-all-start) | async-done | bytes 65568 | tf_op jit(solution)/shard_map/all_to_all | solution.py:410
  38.7 7.0 %shard_map.62 = f32[3,4,128]{2,1,0:T(4,128)} custom-call(s32[4,64]{1,0:T(4,128)S(1)} %fusion.9.index, s32[4]{0:T(128)S(1)} %copy-done.2, s32[3]{0:T(128)S(1)} %pad_add_fusion.place, f32[4,8,128]{2,1,0:T(8,128)S(1)} %shard_map.59.own_ref, f32[32,4,128]{2,1,0:T(4,128)} %get-tuple-element.8.weight_own, f32[4,8,128]{2,1,0:T(8,128)S(1)} %get-tuple-element.9.part, ...), custom_call_target="tpu_custom_call" | custom-call | flops 4000000000 | bytes 4000000 | tf_op jit(solution)/shard_map/pallas_call | solution.py:339
  (9 shorter events, 0.1 us)
Async XLA Ops:
  0.6 0.7 %copy-start = (f32[4,5,128]{2,0,1:T(4,128)S(1)}, f32[4,5,128]{2,0,1:T(4,128)}, u32[]{:S(2)}) copy-start(f32[4,5,128]{2,0,1:T(4,128)} %param.4) | copy-start | bytes 30724
  1.3 12.4 %copy-start.3 = (s32[4,64]{1,0:T(4,128)S(1)}, s32[4,64]{1,0:T(4,128)}, u32[]{:S(2)}) copy-start(s32[4,64]{1,0:T(4,128)} %param.6) | copy-start | bytes 3076
  1.3 16.6 %copy-start.1 = (f32[4,128]{1,0:T(4,128)S(1)}, f32[4,128]{1,0:T(4,128)}, u32[]{:S(2)}) copy-start(f32[4,128]{1,0:T(4,128)} %entropy.1) | copy-start | bytes 6148
  1.3 16.6 %copy-start.2 = (s32[4]{0:T(128)S(1)}, s32[4]{0:T(128)}, u32[]{:S(2)}) copy-start(s32[4]{0:T(128)} %counts.5) | copy-start | bytes 52
  1.4 7.0 %collective-permute-start.2 = (f32[4,8,128]{2,1,0:T(8,128)S(1)}, f32[4,8,128]{2,1,0:T(8,128)S(1)}, u32[]{:S(2)}, u32[]{:S(2)}) collective-permute-start(f32[4,8,128]{2,1,0:T(8,128)S(1)} %shard_map.59.own_ref), channel_id=1, source_target_pairs={{0,2},{2,4},{4,6},{6,0},{1,3},{3,5},{5,7},{7,1},{8,10},{10,12},{12... | collective-permute-start | bytes 49160 | tf_op jit(solution)/shard_map/ppermute | solution.py:368
  4.5 4.7 %collective-permute-start.1 = (f32[4,8,128]{2,1,0:T(8,128)S(1)}, f32[4,8,128]{2,1,0:T(8,128)S(1)}, u32[]{:S(2)}, u32[]{:S(2)}) collective-permute-start(f32[4,8,128]{2,1,0:T(8,128)S(1)} %shard_map.59.own_ref), channel_id=1, source_target_pairs={{0,4},{2,6},{4,0},{6,2},{1,5},{3,7},{5,1},{7,3},{8,12},{10,14},{12... | collective-permute-start | bytes 49160 | tf_op jit(solution)/shard_map/ppermute | solution.py:368
  7.1 3.7 %collective-permute-start = (f32[4,8,128]{2,1,0:T(8,128)S(1)}, f32[4,8,128]{2,1,0:T(8,128)S(1)}, u32[]{:S(2)}, u32[]{:S(2)}) collective-permute-start(f32[4,8,128]{2,1,0:T(8,128)S(1)} %shard_map.59.own_ref), channel_id=1, source_target_pairs={{0,6},{2,0},{4,2},{6,4},{1,7},{3,1},{5,3},{7,5},{8,14},{10,8},{12,... | collective-permute-start | bytes 49160 | tf_op jit(solution)/shard_map/ppermute | solution.py:368
  10.8 5.2 %collective-permute-start.3 = (f32[16,8,128]{2,1,0:T(8,128)S(1)}, f32[16,8,128]{2,1,0:T(8,128)S(1)}, u32[]{:S(2)}, u32[]{:S(2)}) collective-permute-start(f32[16,8,128]{2,1,0:T(8,128)S(1)} %pad_maximum_fusion.rest_2_), channel_id=1, source_target_pairs={{0,8},{8,16},{16,24},{24,0},{1,9},{9,17},{17,25},{25,1},{2,10},{10... | collective-permute-start | bytes 196616 | tf_op jit(solution)/shard_map/ppermute | solution.py:368
  12.3 4.4 %collective-permute-start.6 = (f32[16,8,128]{2,1,0:T(8,128)S(1)}, f32[16,8,128]{2,1,0:T(8,128)S(1)}, u32[]{:S(2)}, u32[]{:S(2)}) collective-permute-start(f32[16,8,128]{2,1,0:T(8,128)S(1)} %pad_maximum_fusion.rest_2_), channel_id=1, source_target_pairs={{0,24},{8,0},{16,8},{24,16},{1,25},{9,1},{17,9},{25,17},{2,26},{10... | collective-permute-start | bytes 196616 | tf_op jit(solution)/shard_map/ppermute | solution.py:368
  13.8 3.0 %collective-permute-start.5 = (f32[16,8,128]{2,1,0:T(8,128)S(1)}, f32[16,8,128]{2,1,0:T(8,128)S(1)}, u32[]{:S(2)}, u32[]{:S(2)}) collective-permute-start(f32[16,8,128]{2,1,0:T(8,128)S(1)} %pad_maximum_fusion.rest_2_), channel_id=1, source_target_pairs={{0,1},{1,0},{2,3},{3,2},{4,5},{5,4},{6,7},{7,6},{8,9},{9,8},{10,11... | collective-permute-start | bytes 196616 | tf_op jit(solution)/shard_map/ppermute | solution.py:368
  16.0 1.3 %collective-permute-start.4 = (f32[16,8,128]{2,1,0:T(8,128)S(1)}, f32[16,8,128]{2,1,0:T(8,128)S(1)}, u32[]{:S(2)}, u32[]{:S(2)}) collective-permute-start(f32[16,8,128]{2,1,0:T(8,128)S(1)} %collective-permute-done.3.rest_0_), channel_id=1, source_target_pairs={{0,1},{1,0},{2,3},{3,2},{4,5},{5,4},{6,7},{7,6},{8,9},{9,8},{10,11... | collective-permute-start | bytes 196616 | tf_op jit(solution)/shard_map/ppermute | solution.py:368
  16.7 1.3 %collective-permute-start.7 = (f32[16,8,128]{2,1,0:T(8,128)S(1)}, f32[16,8,128]{2,1,0:T(8,128)S(1)}, u32[]{:S(2)}, u32[]{:S(2)}) collective-permute-start(f32[16,8,128]{2,1,0:T(8,128)S(1)} %collective-permute-done.6.rest_4_), channel_id=1, source_target_pairs={{0,1},{1,0},{2,3},{3,2},{4,5},{5,4},{6,7},{7,6},{8,9},{9,8},{10,11... | collective-permute-start | bytes 196616 | tf_op jit(solution)/shard_map/ppermute | solution.py:368
  25.2 13.5 %all-to-all-start = ((f32[32,4,128]{2,1,0:T(4,128)}), f32[32,4,128]{2,1,0:T(4,128)S(1)}, u32[]{:S(2)}, u32[]{:S(2)}) async-start(f32[32,4,128]{2,1,0:T(4,128)} %get-tuple-element.8.weight_own), calls=%async_computation | async-start | bytes 131072 | tf_op jit(solution)/shard_map/all_to_all | solution.py:410
